TPU v7x, 128 devices: a whole 4x4x4 slice. The times are simulated.
128 devices in a mesh: dp: 8 (over x_lo, z), cell: 16 (over x_hi, y, core).
Axes of the slice: x: 4 (x_hi: 2, x_lo: 2; x = x_hi * 2 + x_lo), y: 4, z: 4, core: 2. Of those that a mesh axis runs over, the one named last changes fastest.
Arguments:
- sensitivity: float32 [4096, 65536], P(('dp', 'cell')), may hold values from -0.09375 to 0.09375
- row_period: int32 [4096], P(('dp', 'cell')), may hold values from 0 to 31
- row_site: int32 [4096], P(('dp', 'cell')), may hold values from 0 to 127
- period_err: float32 [32], replicated, may hold values from 0.2 to 2
- site_err: float32 [128], replicated, may hold values from 0.2 to 2
- cell_var: float32 [65536], replicated, may hold values from 0.25 to 4
- cell_perm: int32 [65536], replicated, may hold values from 0 to 65535, each once
Outputs:
- gram: float32 [4096, 4096], P('cell', 'dp')
Inputs may be any that keep to these rules, and one draw needn't show every extreme that they name: `cell_perm`: a permutation of 0 to 65535.
All inputs are finite; a program needn't handle non-finite values.
Results may differ from a plain program's by a relative error of at most 0.0009.
Values may be sent and summed in bfloat16 or wider, within the bound.
No kernel may reach another device: no remote copies, remote signals or barrier semaphores. Data moves between devices by JAX's collectives and lax.ppermute only.
A program may use at most 128 MiB of HBM per device.

v0:
```python
import jax
import jax.numpy as jnp
from jax import lax
from jax.sharding import PartitionSpec as P


def pack_rows(sensitivity, row_period, row_site, period_err, site_err):
    period_hit = row_period[:, None] == jnp.arange(period_err.shape[0], dtype=jnp.int32)[None, :]
    site_hit = row_site[:, None] == jnp.arange(site_err.shape[0], dtype=jnp.int32)[None, :]
    period_scale = jnp.sum(jnp.where(period_hit, period_err[None, :], 0.0), axis=1)
    site_scale = jnp.sum(jnp.where(site_hit, site_err[None, :], 0.0), axis=1)
    row_weight = 1.0 / jnp.sqrt(period_scale * period_scale + site_scale * site_scale)
    return (row_weight[:, None] * sensitivity).astype(jnp.bfloat16)


def weigh_columns(scaled, cell_var, cell_perm, first_cell):
    width = scaled.shape[1]
    positions = lax.dynamic_slice_in_dim(cell_perm, first_cell, width)
    column_var = cell_var[positions]
    return (scaled.astype(jnp.float32) * column_var[None, :]).astype(jnp.bfloat16)


def against(rows_block, weighted):
    return lax.dot_general(
        rows_block, weighted, (((1,), (1,)), ((), ())), preferred_element_type=jnp.float32
    )


def body(sensitivity, row_period, row_site, period_err, site_err, cell_var, cell_perm):
    packed = pack_rows(sensitivity, row_period, row_site, period_err, site_err)
    total_cells = cell_var.shape[0]
    scaled = lax.all_to_all(packed, "cell", split_axis=1, concat_axis=0, tiled=True)
    first_cell = lax.axis_index("cell") * (total_cells // lax.axis_size("cell"))
    weighted = weigh_columns(scaled, cell_var, cell_perm, first_cell)
    partial_value = against(lax.all_gather(scaled, "dp", axis=0, tiled=True), weighted)
    gram = lax.psum_scatter(partial_value, "cell", scatter_dimension=0, tiled=True)
    return gram


def solution(mesh):
    return jax.shard_map(
        body,
        mesh=mesh,
        in_specs=(
            P(("dp", "cell"), None),
            P(("dp", "cell")),
            P(("dp", "cell")),
            P(),
            P(),
            P(),
            P(),
        ),
        out_specs=P("cell", "dp"),
        check_vma=False,
    )
```

profile of v0, /device:TPU:0, one launch (start us, length us, event | category | flops | bytes accessed | tf_op | source)
XLA Modules:
  0.0 530.3 jit_solution(9039433479260723975)
XLA Ops:
  6.5 0.0 copy-start
  6.5 0.0 all-gather.2.cloned.1.call-start
  6.5 0.9 select_reduce_fusion.1
  7.4 0.9 select_reduce_fusion
  8.3 3.9 multiply_convert_fusion.1
  12.2 0.3 copy.13
  12.5 58.7 %all_to_all.19 = bf16[32,16,4096]{2,0,1:T(8,128)(2,1)} all-to-all(bf16[32,16,4096]{2,0,1:T(8,128)(2,1)S(1)} %bitcast.11), channel_id=1, replica_groups=mesh['dp'=8,'cell'=16] {'cell'}, dimensions={1} | all-to-all | bytes 8388608 | tf_op jit(solution)/shard_map/all_to_all | solution.py:32
  71.2 0.0 all-gather.2.cloned.1.call-update
  71.2 0.0 reduce-scatter.2.cloned.1.call-start
  71.3 0.7 fusion.2
  72.0 0.0 copy-done
  72.0 23.0 %gather_fusion = f32[4096]{0:T(1024)S(1)} fusion(f32[65536]{0:T(1024)S(1)} %copy-done, s32[4096]{0:T(1024)S(1)} %fusion.2), kind=kCustom, calls=%fused_computation | custom fusion | bytes 49152 | tf_op jit(solution)/shard_map/gather | solution.py:19
  95.1 302.5 %all-gather.2.cloned.1.call-done = bf16[4096,4096]{1,0:T(8,128)(2,1)} async-done(((bf16[512,4096]{1,0:T(8,128)(2,1)}), bf16[4096,4096]{1,0:T(8,128)(2,1)}) %all-gather.2.cloned.1.call-update) | async-done | bytes 33554448 | tf_op jit(solution)/shard_map/all_gather | solution.py:35
  397.5 25.0 %fusion = f32[4096,512]{1,0:T(8,128)} fusion(bf16[4096,4096]{1,0:T(8,128)(2,1)} %all-gather.2.cloned.1.call-done, bf16[512,4096]{1,0:T(8,128)(2,1)} %bitcast.9, f32[4096]{0:T(1024)S(1)} %gather_fusion), kind=kOutput, calls=%fused_computation.3 | convolution fusion | flops 17186160640 | bytes 46153728 | tf_op jit(solution)/shard_map/dot_general | solution.py:24
  422.5 0.0 reduce-scatter.2.cloned.1.call-update
  422.5 101.0 %reduce-scatter.2.cloned.1.call-done = f32[256,512]{1,0:T(8,128)} async-done(((f32[4096,512]{1,0:T(8,128)}), f32[256,512]{1,0:T(8,128)}) %reduce-scatter.2.cloned.1.call-update) | async-done | bytes 524304 | tf_op jit(solution)/shard_map/reduce_scatter | solution.py:36
  (1 shorter events, 0.0 us)
Async XLA Ops:
  6.5 65.5 %copy-start = (f32[65536]{0:T(1024)S(1)}, f32[65536]{0:T(1024)}, u32[]{:S(2)}) copy-start(f32[65536]{0:T(1024)} %param.12) | copy-start | bytes 786436
  6.5 391.0 %all-gather.2.cloned.1.call-start = ((), (), s32[]{:S(2)}) async-start(), calls=%async_computation.2 | async-start | bytes 37748736 | tf_op jit(solution)/shard_map/all_gather | solution.py:35
  71.2 452.3 %reduce-scatter.2.cloned.1.call-start = ((), (), s32[]{:S(2)}) async-start(), calls=%async_computation.3 | async-start | bytes 8912896 | tf_op jit(solution)/shard_map/reduce_scatter | solution.py:36
Sparse Core Ops, SparseCore 0:
  71.4 326.1 all-gather.1
  422.7 100.7 reduce-scatter.1
where the time goes:
time: 531 us; the launch traced here: 530 us
  waiting for transfers between devices  403 us (76%)
  blocking collectives  58.7 us (11%)
  matrix products  25 us (5%)
  local copies, waits for them, and re-layouts  23.3 us (4%)
  between operations  13.4 us (3%)
  other arithmetic  6.41 us (1%)
    all_gather x1, waiting for transfers between devices, body(): lax.all_gather(scaled, 'dp', axis=0, tiled=True)  302 us
    reduce_scatter x1, waiting for transfers between devices, body(): lax.psum_scatter(partial_value, 'cell', scatter_dimension=0, tiled=True)  101 us
    all_to_all x1, blocking collectives, body(): lax.all_to_all(packed, 'cell', split_axis=1, concat_axis=0, tiled=True)  58.7 us
    dot_general x1, matrix products, against(): lax.dot_general(rows_block, weighted, (((1,), (1,)), ((), ())), preferred...  25 us
    gather x1, local copies, waits for them, and re-layouts, weigh_columns(): column_var = cell_var[positions]  23 us
  transfers between devices with their start and end apart: 2, of which 2 were waited for; matrix products, arithmetic and copies ran while one was open for 4% of the time, Pallas kernels for 0%

commit v1 on v0

--- a/solution.py
+++ b/solution.py
@@ -2,6 +2,11 @@
 import jax.numpy as jnp
 from jax import lax
 from jax.sharding import PartitionSpec as P
+
+
+def swapped_in(x, axis, d):
+    sent = jnp.stack([x] * lax.axis_size(axis))
+    return jnp.concatenate(lax.all_to_all(sent, axis, 0, 0), axis=d)
 
 
 def pack_rows(sensitivity, row_period, row_site, period_err, site_err):
@@ -32,7 +37,7 @@
     scaled = lax.all_to_all(packed, "cell", split_axis=1, concat_axis=0, tiled=True)
     first_cell = lax.axis_index("cell") * (total_cells // lax.axis_size("cell"))
     weighted = weigh_columns(scaled, cell_var, cell_perm, first_cell)
-    partial_value = against(lax.all_gather(scaled, "dp", axis=0, tiled=True), weighted)
+    partial_value = against(swapped_in(scaled, "dp", 0), weighted)
     gram = lax.psum_scatter(partial_value, "cell", scatter_dimension=0, tiled=True)
     return gram
 

time: 531 us -> 586 us (1.10)
  waiting for transfers between devices: 403 us -> 433 us
  local copies, waits for them, and re-layouts: 23.3 us -> 36.2 us
  starting transfers between devices: 0.04 us -> 7.1 us
    all_to_all x0 -> x1, waiting for transfers between devices: none -> 335 us  [swapped_in(): return jnp.concatenate(lax.all_to_all(sent, axis, 0, 0), axis=d)]
    all_gather x1 -> x0, waiting for transfers between devices: 302 us -> none  [body(): lax.all_gather(scaled, 'dp', axis=0, tiled=True)]
    another operation x0 -> x1, local copies, waits for them, and re-layouts: none -> 10.9 us  [swapped_in(): sent = jnp.stack([x] * lax.axis_size(axis))]
    all_to_all x0 -> x1, starting transfers between devices: none -> 7.06 us  [swapped_in(): return jnp.concatenate(lax.all_to_all(sent, axis, 0, 0), axis=d)]
  transfers between devices with their start and end apart: 2 -> 2, of which waited for: 2 -> 2; matrix products, arithmetic and copies ran while one was open for 4% -> 5% of each run, Pallas kernels for 0% -> 0%
where the time goes in v1:
time: 586 us; the launch traced here: 585 us
  waiting for transfers between devices  433 us (74%)
  blocking collectives  58.6 us (10%)
  local copies, waits for them, and re-layouts  36.2 us (6%)
  matrix products  25 us (4%)
  between operations  13.4 us (2%)
  other arithmetic  11.7 us (2%)
  starting transfers between devices  7.1 us (1%)
    all_to_all x1, waiting for transfers between devices, swapped_in(): return jnp.concatenate(lax.all_to_all(sent, axis, 0, 0), axis=d)  335 us
    reduce_scatter x1, waiting for transfers between devices, body(): lax.psum_scatter(partial_value, 'cell', scatter_dimension=0, tiled=True)  98.7 us
    all_to_all x1, blocking collectives, body(): lax.all_to_all(packed, 'cell', split_axis=1, concat_axis=0, tiled=True)  58.6 us
    dot_general x1, matrix products, against(): lax.dot_general(rows_block, weighted, (((1,), (1,)), ((), ())), preferred...  25 us
    gather x1, local copies, waits for them, and re-layouts, weigh_columns(): column_var = cell_var[positions]  23 us
  transfers between devices with their start and end apart: 2, of which 2 were waited for; matrix products, arithmetic and copies ran while one was open for 5% of the time, Pallas kernels for 0%

profile of v1, /device:TPU:0, one launch (start us, length us, event | category | flops | bytes accessed | tf_op | source)
XLA Modules:
  0.0 585.4 jit_solution(14647596916848780406)
XLA Ops:
  6.5 0.0 copy-start
  6.5 0.9 select_reduce_fusion.1
  7.4 0.9 select_reduce_fusion
  8.3 3.9 multiply_convert_fusion.1
  12.2 0.3 copy.14
  12.5 58.6 %all_to_all.21 = bf16[32,16,4096]{2,0,1:T(8,128)(2,1)S(1)} all-to-all(bf16[32,16,4096]{2,0,1:T(8,128)(2,1)S(1)} %bitcast.14), channel_id=1, replica_groups=mesh['dp'=8,'cell'=16] {'cell'}, dimensions={1} | all-to-all | bytes 8388608 | tf_op jit(solution)/shard_map/all_to_all | solution.py:37
  71.1 0.0 copy-start.2
  71.1 1.9 copy-done.2
  73.0 10.9 %stack.5 = bf16[8,512,4096]{2,1,0:T(8,128)(2,1)} broadcast(bf16[512,4096]{1,0:T(8,128)(2,1)S(1)} %bitcast.12), dimensions={1,2} | broadcast | bytes 37748736 | tf_op jit(solution)/shard_map/stack | solution.py:8
  84.0 7.1 %all-to-all-start.1 = ((bf16[8,512,4096]{2,1,0:T(8,128)(2,1)}), bf16[8,512,4096]{2,1,0:T(8,128)(2,1)}, u32[]{:S(2)}, u32[]{:S(2)}) async-start(bf16[8,512,4096]{2,1,0:T(8,128)(2,1)} %stack.5), calls=%async_computation.1 | async-start | bytes 67108864 | tf_op jit(solution)/shard_map/all_to_all | solution.py:9
  91.0 0.0 reduce-scatter.2.cloned.1.call-start
  91.1 0.7 fusion
  91.8 0.0 copy-done
  91.8 23.0 %gather_fusion = f32[4096]{0:T(1024)S(1)} fusion(f32[65536]{0:T(1024)S(1)} %copy-done, s32[4096]{0:T(1024)S(1)} %fusion), kind=kCustom, calls=%fused_computation | custom fusion | bytes 49152 | tf_op jit(solution)/shard_map/gather | solution.py:24
  114.9 5.3 multiply_convert_fusion
  120.1 334.7 %all-to-all-done.1 = bf16[8,512,4096]{2,1,0:T(8,128)(2,1)} async-done(((bf16[8,512,4096]{2,1,0:T(8,128)(2,1)}), bf16[8,512,4096]{2,1,0:T(8,128)(2,1)}, u32[]{:S(2)}, u32[]{:S(2)}) %all-to-all-start.1) | async-done | bytes 33554464 | tf_op jit(solution)/shard_map/all_to_all | solution.py:9
  454.8 0.0 copy-start.1
  454.8 25.0 %fusion.1 = f32[4096,512]{1,0:T(8,128)} fusion(bf16[4096,4096]{1,0:T(8,128)(2,1)} %bitcast.2, bf16[512,4096]{1,0:T(8,128)(2,1)} %bitcast.15), kind=kOutput, calls=%fused_computation.11 | convolution fusion | flops 17179869184 | bytes 46137344 | tf_op jit(solution)/shard_map/dot_general | solution.py:29
  479.8 0.0 reduce-scatter.2.cloned.1.call-update
  479.9 98.7 %reduce-scatter.2.cloned.1.call-done = f32[256,512]{1,0:T(8,128)} async-done(((f32[4096,512]{1,0:T(8,128)}), f32[256,512]{1,0:T(8,128)}) %reduce-scatter.2.cloned.1.call-update) | async-done | bytes 524304 | tf_op jit(solution)/shard_map/reduce_scatter | solution.py:41
  578.6 0.0 copy-done.1
  (1 shorter events, 0.0 us)
Async XLA Ops:
  6.5 85.3 %copy-start = (f32[65536]{0:T(1024)S(1)}, f32[65536]{0:T(1024)}, u32[]{:S(2)}) copy-start(f32[65536]{0:T(1024)} %param.12) | copy-start | bytes 786436
  71.1 1.9 copy-start.2
  84.0 370.8 %all-to-all-start.1 = ((bf16[8,512,4096]{2,1,0:T(8,128)(2,1)}), bf16[8,512,4096]{2,1,0:T(8,128)(2,1)}, u32[]{:S(2)}, u32[]{:S(2)}) async-start(bf16[8,512,4096]{2,1,0:T(8,128)(2,1)} %stack.5), calls=%async_computation.1 | async-start | bytes 67108864 | tf_op jit(solution)/shard_map/all_to_all | solution.py:9
  91.0 487.5 %reduce-scatter.2.cloned.1.call-start = ((), (), s32[]{:S(2)}) async-start(), calls=%async_computation.3 | async-start | bytes 8912896 | tf_op jit(solution)/shard_map/reduce_scatter | solution.py:41
  454.8 123.8 %copy-start.1 = (f32[65536]{0:T(1024)S(1)}, f32[65536]{0:T(1024)}, u32[]{:S(2)}) copy-start(f32[65536]{0:T(1024)} %param.12) | copy-start | bytes 786436
Sparse Core Ops, SparseCore 0:
  480.0 98.5 reduce-scatter.1
